TPU v7x, 256 devices: a whole 4x4x8 slice. The times are simulated.
256 devices in a mesh: rows: 32 (over z, y), samp: 8 (over x, core).
Axes of the slice: x: 4, y: 4, z: 8, core: 2. Of those that a mesh axis runs over, the one named last changes fastest.
Arguments:
- coupling_tiles: bfloat16 [512, 32, 128, 128], P('rows', 'samp'), may hold values from -0.09375 to 0.09375
- tile_columns: int32 [512, 32], P('rows', 'samp'), may hold values from 0 to 511, as said below
- sample_matrix: bfloat16 [65536, 512], P('rows'), may hold values from -6 to 6
- phi_leaf: float32 [512, 256], replicated, may hold values from -0.25 to 0.25
- phi_pair: float32 [512, 256], replicated, may hold values from -0.25 to 0.25
- phi_quad: float32 [512, 256], replicated, may hold values from -0.25 to 0.25
Outputs:
- leaf_basis: float32 [65536, 256], P('rows')
- nested_transfer: float32 [8192, 256], P('rows')
- sample_approx: float32 [65536, 512], P('rows', 'samp')
Inputs may be any that keep to these rules, and one draw needn't show every extreme that they name: `tile_columns`: the 32 tile columns of a tile row are distinct and lie in the leaf block of that row or in one of the two leaf blocks beside it (16 tile rows to a leaf block).
All inputs are finite; a program needn't handle non-finite values.
Results may differ from a plain program's by a relative error of at most 0.0003.
Values may be sent and summed in bfloat16 or wider, within the bound.
A program may use at most 128 MiB of HBM per device.

v0:
```python
import jax
import jax.numpy as jnp
from jax import lax
from jax.sharding import PartitionSpec as P

NS_ITERS = 5
HIGH = lax.Precision.HIGHEST


def with_halo(block, sides, width):
    for axis, dim in sides:
        count = lax.axis_size(axis)
        forward = [(i, i + 1) for i in range(count - 1)]
        backward = [(target, source) for source, target in forward]
        low = lax.ppermute(
            lax.slice_in_dim(block, block.shape[dim] - width, None, axis=dim), axis, forward
        )
        high = lax.ppermute(lax.slice_in_dim(block, 0, width, axis=dim), axis, backward)
        block = jnp.concatenate([low, block, high], axis=dim)
    return block


def swapped(value, axis, distance):
    return lax.ppermute(value, axis, [(i, i ^ 1 << distance) for i in range(lax.axis_size(axis))])


def product(left, right):
    return jnp.dot(left, right, precision=HIGH, preferred_element_type=jnp.float32)


def orthogonal(matrix):
    gram_matrix = product(matrix.T, matrix)
    norm_scale = jnp.sqrt(jnp.sum(gram_matrix * gram_matrix)) + 1e-06
    identity = jnp.eye(gram_matrix.shape[0], dtype=jnp.float32)
    iterate = gram_matrix / norm_scale
    inverse_root = identity
    for step in range(NS_ITERS):
        factor = 1.5 * identity - 0.5 * product(inverse_root, iterate)
        iterate = product(iterate, factor)
        inverse_root = product(factor, inverse_root)
    return product(matrix, inverse_root) / jnp.sqrt(norm_scale)


def stack_pair(mine, other, which_bit):
    lower = jnp.where(which_bit == 0, mine, other)
    higher = jnp.where(which_bit == 0, other, mine)
    return jnp.concatenate([lower, higher], axis=0)


def on_device(coupling_tiles, tile_columns, sample_matrix, phi_leaf, phi_pair, phi_quad):
    per_leaf = 16
    leaf_rows = sample_matrix.shape[0]
    sample_cols = sample_matrix.shape[1]
    row_index = lax.axis_index("rows")
    extended = with_halo(sample_matrix, (("rows", 0),), leaf_rows)
    blocks = extended.reshape(3 * per_leaf, leaf_rows // per_leaf, sample_cols)
    local_columns = tile_columns - (row_index - 1) * per_leaf
    picked = jnp.take(blocks, local_columns, axis=0)
    partial_value = jnp.einsum(
        "tkab,tkbs->tas", coupling_tiles, picked, preferred_element_type=jnp.float32
    )
    partial_value = partial_value.reshape(leaf_rows, sample_cols)
    samp_count = lax.axis_size("samp")
    samp_index = lax.axis_index("samp")
    share_cols = sample_cols // samp_count
    sample = lax.psum(partial_value, "samp")

    def sketch(stacked, phi_matrix):
        return product(stacked, phi_matrix)

    def merge_level(stacked, phi_matrix):
        basis_now = orthogonal(sketch(stacked, phi_matrix))
        return (basis_now, product(basis_now.T, stacked))

    basis, coarse = merge_level(sample, phi_leaf)
    sibling_bit = row_index % 2
    cousin_bit = row_index // 2 % 2
    pair = stack_pair(coarse, swapped(coarse, "rows", 0), sibling_bit)
    upper, middle = merge_level(pair, phi_pair)
    quad = stack_pair(middle, swapped(middle, "rows", 1), cousin_bit)
    top, summary = merge_level(quad, phi_quad)
    rank_leaf = coarse.shape[0]
    rank_pair = middle.shape[0]
    own_upper = lax.dynamic_slice_in_dim(upper, sibling_bit * rank_leaf, rank_leaf, 0)
    own_top = lax.dynamic_slice_in_dim(top, cousin_bit * rank_pair, rank_pair, 0)
    nested = product(own_upper, own_top)
    approx = product(
        basis,
        product(nested, lax.dynamic_slice_in_dim(summary, samp_index * share_cols, share_cols, 1)),
    )
    return (basis, nested, approx)


def solution(mesh):
    return jax.shard_map(
        on_device,
        mesh=mesh,
        in_specs=(P("rows", "samp", None, None), P("rows", "samp"), P("rows", None), P(), P(), P()),
        out_specs=(P("rows", None), P("rows", None), P("rows", "samp")),
        check_vma=False,
    )
```

profile of v0, /device:TPU:7, one launch (start us, length us, event | category | flops | bytes accessed | tf_op | source)
XLA Modules:
  0.0 261.3 jit_solution(8823519993755245035)
XLA Ops:
  7.2 4.7 %collective-permute-start = (bf16[2048,512]{1,0:T(8,128)(2,1)}, bf16[2048,512]{1,0:T(8,128)(2,1)}, u32[]{:S(2)}, u32[]{:S(2)}) collective-permute-start(bf16[2048,512]{1,0:T(8,128)(2,1)} %param.8), channel_id=1, source_target_pairs={{0,8},{8,16},{16,24},{24,32},{32,40},{40,48},{48,56},{56,64},{64,7... | collective-permute-start | bytes 6291464 | tf_op jit(solution)/shard_map/ppermute | solution.py:15
  11.9 1.3 collective-permute-start.1
  14.1 41.0 %collective-permute-done = bf16[2048,512]{1,0:T(8,128)(2,1)} collective-permute-done((bf16[2048,512]{1,0:T(8,128)(2,1)}, bf16[2048,512]{1,0:T(8,128)(2,1)}, u32[]{:S(2)}, u32[]{:S(2)}) %collective-permute-start) | collective-permute-done | bytes 2097184 | tf_op jit(solution)/shard_map/ppermute | solution.py:15
  55.2 5.1 %collective-permute-done.1 = bf16[2048,512]{1,0:T(8,128)(2,1)} collective-permute-done((bf16[2048,512]{1,0:T(8,128)(2,1)}, bf16[2048,512]{1,0:T(8,128)(2,1)}, u32[]{:S(2)}, u32[]{:S(2)}) %collective-permute-start.1) | collective-permute-done | bytes 2097184 | tf_op jit(solution)/shard_map/ppermute | solution.py:18
  60.3 6.0 %pad_maximum_fusion = bf16[6144,512]{1,0:T(8,128)(2,1)} fusion(bf16[2048,512]{1,0:T(8,128)(2,1)} %collective-permute-done.1, bf16[2048,512]{1,0:T(8,128)(2,1)} %param.8, bf16[2048,512]{1,0:T(8,128)(2,1)} %collective-permute-done), kind=kLoop, calls=%fused_computation.4 | loop fusion | flops 18874368 | bytes 12582912 | tf_op jit(solution)/shard_map/concatenate | solution.py:19
  66.2 8.3 %gather_fusion = bf16[64,128,512]{2,1,0:T(8,128)(2,1)} fusion(bf16[48,128,512]{2,1,0:T(8,128)(2,1)} %bitcast.104, s32[1024]{0:T(1024)S(1)} %pad_clamp_fusion), kind=kCustom, calls=%fused_computation | custom fusion | bytes 16777472 | tf_op jit(solution)/shard_map/jit(_take)/gather | solution.py:58
  74.6 7.1 %fusion = f32[16,512,128,1]{1,2,3,0:T(8,128)} fusion(bf16[16,4,128,128]{3,2,1,0:T(8,128)(2,1)S(1)} %copy-done, bf16[16,4,128,512]{3,2,1,0:T(8,128)(2,1)} %bitcast.105, pred[16,4]{1,0:T(8,128)(4,1)S(1)} %copy.11), kind=kOutput, calls=%fused_computation.1 | convolution fusion | flops 1077936128 | bytes 14680128 | tf_op jit(solution)/shard_map/tkab,tkbs->tas/dot_general | solution.py:59
  81.7 81.9 %all-reduce.2.cloned.1.call-done = f32[2048,512]{1,0:T(8,128)} async-done(((f32[2048,512]{1,0:T(8,128)}), f32[2048,512]{1,0:T(8,128)}) %all-reduce.2.cloned.1.call-update) | async-done | bytes 4194320 | tf_op jit(solution)/shard_map/psum | solution.py:66
  163.6 5.7 %fusion.26 = f32[2048,256]{1,0:T(8,128)S(1)} fusion(f32[2048,512]{1,0:T(8,128)} %all-reduce.2.cloned.1.call-done, f32[512,256]{1,0:T(8,128)S(1)} %copy-done.11), kind=kOutput, calls=%fused_computation.77 | convolution fusion | flops 3221225472 | bytes 6815744 | tf_op jit(solution)/shard_map/dot_general | solution.py:28
  169.3 1.3 copy-done.1
  170.7 4.2 %multiply_reduce_fusion.2 = (f32[]{:T(128)}, f32[256,256]{1,0:T(8,128)S(1)}) fusion(f32[2048,256]{1,0:T(8,128)S(1)} %fusion.26), kind=kOutput, calls=%fused_computation.50 | convolution fusion | flops 1610743808 | bytes 2359300 | tf_op jit(solution)/shard_map/dot_general | solution.py:28
  180.9 3.7 %convolution_divide_fusion = f32[2048,256]{1,0:T(8,128)S(1)} fusion(f32[2048,256]{1,0:T(8,128)} %copy-done.1, f32[256,256]{1,0:T(8,128)S(1)} %fusion.33, f32[]{:T(128)S(6)} %sqrt.19), kind=kOutput, calls=%fused_computation.6 | convolution fusion | flops 1611137024 | bytes 4456452 | tf_op jit(solution)/shard_map/dot_general | solution.py:28
  184.6 4.0 %fusion.34 = f32[256,512]{1,0:T(8,128)S(1)} fusion(f32[2048,256]{1,0:T(8,128)S(1)} %convolution_divide_fusion, f32[2048,512]{1,0:T(8,128)S(1)} %copy-done.2), kind=kOutput, calls=%fused_computation.85 | convolution fusion | flops 3221225472 | bytes 6815744 | tf_op jit(solution)/shard_map/dot_general | solution.py:28
  188.6 1.3 collective-permute-start.2
  189.9 11.4 %collective-permute-done.2 = f32[256,512]{1,0:T(8,128)} collective-permute-done((f32[256,512]{1,0:T(8,128)S(1)}, f32[256,512]{1,0:T(8,128)}, u32[]{:S(2)}, u32[]{:S(2)}) %collective-permute-start.2) | collective-permute-done | bytes 524320 | tf_op jit(solution)/shard_map/ppermute | solution.py:24
  201.3 1.3 broadcast_select_fusion.3
  202.6 2.0 fusion.7
  205.4 1.6 multiply_reduce_fusion.1
  211.5 1.1 fusion.40
  213.0 1.3 select_subtract_fusion.5
  214.7 1.6 convolution_divide_fusion.2
  216.4 1.9 fusion.6
  218.2 2.9 %collective-permute-start.3 = (f32[256,512]{1,0:T(8,128)}, f32[256,512]{1,0:T(8,128)}, u32[]{:S(2)}, u32[]{:S(2)}) collective-permute-start(f32[256,512]{1,0:T(8,128)} %fusion.6), channel_id=1, source_target_pairs={{0,16},{8,24},{16,0},{24,8},{32,48},{40,56},{48,32},{56,40},{64,80... | collective-permute-start | bytes 1572872 | tf_op jit(solution)/shard_map/ppermute | solution.py:24
  221.1 12.9 %collective-permute-done.3 = f32[256,512]{1,0:T(8,128)} collective-permute-done((f32[256,512]{1,0:T(8,128)}, f32[256,512]{1,0:T(8,128)}, u32[]{:S(2)}, u32[]{:S(2)}) %collective-permute-start.3) | collective-permute-done | bytes 524320 | tf_op jit(solution)/shard_map/ppermute | solution.py:24
  234.1 1.3 broadcast_select_fusion.1
  235.4 2.0 fusion.5
  238.2 1.6 multiply_reduce_fusion
  244.2 1.1 fusion.47
  245.8 1.5 select_subtract_fusion
  247.7 1.6 convolution_divide_fusion.1
  249.3 1.1 fusion.4
  251.2 3.0 %fusion.49 = f32[2048,64]{0,1:T(8,128)} fusion(f32[2048,256]{1,0:T(8,128)S(1)} %copy-done.4, f32[256,64]{1,0:T(8,128)S(1)} %fusion.14), kind=kOutput, calls=%fused_computation.100 | convolution fusion | flops 402653184 | bytes 2686976 | tf_op jit(solution)/shard_map/dot_general | solution.py:28
  (70 shorter events, 17.4 us)
Async XLA Ops:
  7.2 67.4 %copy-start = (bf16[16,4,128,128]{3,2,1,0:T(8,128)(2,1)S(1)}, bf16[16,4,128,128]{3,2,1,0:T(8,128)(2,1)}, u32[]{:S(2)}) copy-start(bf16[16,4,128,128]{3,2,1,0:T(8,128)(2,1)} %param.6) | copy-start | bytes 6291460
  7.2 156.4 %all-reduce.2.cloned.1.call-start = ((), (), s32[]{:S(2)}) async-start(), calls=%async_computation | async-start | bytes 8388608 | tf_op jit(solution)/shard_map/psum | solution.py:66
  7.2 47.9 %collective-permute-start = (bf16[2048,512]{1,0:T(8,128)(2,1)}, bf16[2048,512]{1,0:T(8,128)(2,1)}, u32[]{:S(2)}, u32[]{:S(2)}) collective-permute-start(bf16[2048,512]{1,0:T(8,128)(2,1)} %param.8), channel_id=1, source_target_pairs={{0,8},{8,16},{16,24},{24,32},{32,40},{40,48},{48,56},{56,64},{64,7... | collective-permute-start | bytes 6291464 | tf_op jit(solution)/shard_map/ppermute | solution.py:15
  11.9 48.4 %collective-permute-start.1 = (bf16[2048,512]{1,0:T(8,128)(2,1)}, bf16[2048,512]{1,0:T(8,128)(2,1)}, u32[]{:S(2)}, u32[]{:S(2)}) collective-permute-start(bf16[2048,512]{1,0:T(8,128)(2,1)} %param.8), channel_id=1, source_target_pairs={{8,0},{16,8},{24,16},{32,24},{40,32},{48,40},{56,48},{64,56},{72,6... | collective-permute-start | bytes 6291464 | tf_op jit(solution)/shard_map/ppermute | solution.py:18
  81.7 82.0 %copy-start.11 = (f32[512,256]{1,0:T(8,128)S(1)}, f32[512,256]{1,0:T(8,128)}, u32[]{:S(2)}) copy-start(f32[512,256]{1,0:T(8,128)} %param.9) | copy-start | bytes 1572868
  169.3 1.3 copy-start.1
  180.5 4.1 %copy-start.2 = (f32[2048,512]{1,0:T(8,128)S(1)}, f32[2048,512]{1,0:T(8,128)}, u32[]{:S(2)}) copy-start(f32[2048,512]{1,0:T(8,128)} %all-reduce.2.cloned.1.call-done) | copy-start | bytes 12582916
  184.6 4.0 %copy-start.3 = (f32[2048,256]{1,0:T(8,128)}, f32[2048,256]{1,0:T(8,128)S(1)}, u32[]{:S(2)}) copy-start(f32[2048,256]{1,0:T(8,128)S(1)} %convolution_divide_fusion) | copy-start | bytes 6291460
  188.6 1.3 copy-start.7
  188.6 12.7 %collective-permute-start.2 = (f32[256,512]{1,0:T(8,128)S(1)}, f32[256,512]{1,0:T(8,128)}, u32[]{:S(2)}, u32[]{:S(2)}) collective-permute-start(f32[256,512]{1,0:T(8,128)S(1)} %fusion.34), channel_id=1, source_target_pairs={{0,8},{8,0},{16,24},{24,16},{32,40},{40,32},{48,56},{56,48},{64,72... | collective-permute-start | bytes 1572872 | tf_op jit(solution)/shard_map/ppermute | solution.py:24
  204.6 0.8 copy-start.6
  216.3 1.9 copy-start.8
  218.2 15.9 %collective-permute-start.3 = (f32[256,512]{1,0:T(8,128)}, f32[256,512]{1,0:T(8,128)}, u32[]{:S(2)}, u32[]{:S(2)}) collective-permute-start(f32[256,512]{1,0:T(8,128)} %fusion.6), channel_id=1, source_target_pairs={{0,16},{8,24},{16,0},{24,8},{32,48},{40,56},{48,32},{56,40},{64,80... | collective-permute-start | bytes 1572872 | tf_op jit(solution)/shard_map/ppermute | solution.py:24
  237.4 0.8 copy-start.5
  245.8 4.6 %copy-start.9 = (f32[512,256]{1,0:T(8,128)S(1)}, f32[512,256]{1,0:T(8,128)}, u32[]{:S(2)}) copy-start(f32[512,256]{1,0:T(8,128)} %copy-done.8) | copy-start | bytes 1572868
  245.8 5.5 %copy-start.4 = (f32[2048,256]{1,0:T(8,128)S(1)}, f32[2048,256]{1,0:T(8,128)}, u32[]{:S(2)}) copy-start(f32[2048,256]{1,0:T(8,128)} %copy-done.3) | copy-start | bytes 6291460
  250.8 3.5 %copy-start.10 = (f32[256,256]{1,0:T(8,128)}, f32[256,256]{1,0:T(8,128)S(1)}, u32[]{:S(2)}) copy-start(f32[256,256]{1,0:T(8,128)S(1)} %fusion.8) | copy-start | bytes 786436
Sparse Core Ops, SparseCore 0:
  81.8 81.7 all-reduce.1
where the time goes:
time: 266 us; the launch traced here: 261 us
  waiting for transfers between devices  152 us (57%)
  matrix products  60.9 us (23%)
  between operations  17 us (6%)
  local copies, waits for them, and re-layouts  11.5 us (4%)
  starting transfers between devices  10.2 us (4%)
  other arithmetic  9.28 us (3%)
    psum x1, waiting for transfers between devices, on_device(): sample = lax.psum(partial_value, 'samp')  81.9 us
    dot_general x57, matrix products, product(): jnp.dot(left, right, precision=HIGH, preferred_element_type=jnp.float32)  53.8 us
    ppermute x1, waiting for transfers between devices, with_halo(): lax.ppermute(lax.slice_in_dim(block, block.shape[dim] - width, None, axis...  41 us
    ppermute x2, waiting for transfers between devices, swapped(): lax.ppermute(value, axis, [(i, i ^ 1 << distance) for i in range(lax.axis...  24.3 us
    gather x1, local copies, waits for them, and re-layouts, on_device(): picked = jnp.take(blocks, local_columns, axis=0)  8.31 us
    dot_general x1, matrix products, on_device(): jnp.einsum('tkab,tkbs->tas', coupling_tiles, picked, preferred_element_ty...  7.1 us
    concatenate x1, other arithmetic, with_halo(): block = jnp.concatenate([low, block, high], axis=dim)  5.99 us
  transfers between devices with their start and end apart: 5, of which 5 were waited for; matrix products, arithmetic and copies ran while one was open for 0% of the time, Pallas kernels for 0%

commit v1 on v0

--- a/solution.py
+++ b/solution.py
@@ -63,7 +63,7 @@
     samp_count = lax.axis_size("samp")
     samp_index = lax.axis_index("samp")
     share_cols = sample_cols // samp_count
-    sample = lax.psum(partial_value, "samp")
+    sample = jnp.sum(lax.all_gather(partial_value, "samp"), axis=0)
 
     def sketch(stacked, phi_matrix):
         return product(stacked, phi_matrix)

time: 266 us -> 355 us (1.33)
  the two profiles are of different devices: /device:TPU:7 before, /device:TPU:2 now
where the time goes in v1:
time: 355 us; the launch traced here: 350 us
  waiting for transfers between devices  233 us (66%)
  matrix products  57.7 us (16%)
  other arithmetic  22 us (6%)
  between operations  17 us (5%)
  starting transfers between devices  11.1 us (3%)
  local copies, waits for them, and re-layouts  8.64 us (2%)
    all_gather x1, waiting for transfers between devices, on_device(): sample = jnp.sum(lax.all_gather(partial_value, 'samp'), axis=0)  162 us
    dot_general x57, matrix products, product(): jnp.dot(left, right, precision=HIGH, preferred_element_type=jnp.float32)  50.5 us
    ppermute x1, waiting for transfers between devices, with_halo(): lax.ppermute(lax.slice_in_dim(block, block.shape[dim] - width, None, axis...  41.6 us
    ppermute x2, waiting for transfers between devices, swapped(): lax.ppermute(value, axis, [(i, i ^ 1 << distance) for i in range(lax.axis...  24.4 us
    reduce_sum x1, other arithmetic, on_device(): sample = jnp.sum(lax.all_gather(partial_value, 'samp'), axis=0)  15.1 us
    gather x1, local copies, waits for them, and re-layouts, on_device(): picked = jnp.take(blocks, local_columns, axis=0)  8.32 us
    dot_general x1, matrix products, on_device(): jnp.einsum('tkab,tkbs->tas', coupling_tiles, picked, preferred_element_ty...  7.19 us
  transfers between devices with their start and end apart: 5, of which 5 were waited for; matrix products, arithmetic and copies ran while one was open for 0% of the time, Pallas kernels for 0%

profile of v1, /device:TPU:2, one launch (start us, length us, event | category | flops | bytes accessed | tf_op | source)
XLA Modules:
  0.0 350.0 jit_solution(13682694166665754532)
XLA Ops:
  7.2 4.9 %collective-permute-start = (bf16[2048,512]{1,0:T(8,128)(2,1)}, bf16[2048,512]{1,0:T(8,128)(2,1)}, u32[]{:S(2)}, u32[]{:S(2)}) collective-permute-start(bf16[2048,512]{1,0:T(8,128)(2,1)} %param.8), channel_id=1, source_target_pairs={{0,8},{8,16},{16,24},{24,32},{32,40},{40,48},{48,56},{56,64},{64,7... | collective-permute-start | bytes 6291464 | tf_op jit(solution)/shard_map/ppermute | solution.py:15
  12.2 1.3 collective-permute-start.1
  13.5 0.7 compare_and_fusion
  14.4 41.6 %collective-permute-done = bf16[2048,512]{1,0:T(8,128)(2,1)} collective-permute-done((bf16[2048,512]{1,0:T(8,128)(2,1)}, bf16[2048,512]{1,0:T(8,128)(2,1)}, u32[]{:S(2)}, u32[]{:S(2)}) %collective-permute-start) | collective-permute-done | bytes 2097184 | tf_op jit(solution)/shard_map/ppermute | solution.py:15
  56.0 5.4 %collective-permute-done.1 = bf16[2048,512]{1,0:T(8,128)(2,1)} collective-permute-done((bf16[2048,512]{1,0:T(8,128)(2,1)}, bf16[2048,512]{1,0:T(8,128)(2,1)}, u32[]{:S(2)}, u32[]{:S(2)}) %collective-permute-start.1) | collective-permute-done | bytes 2097184 | tf_op jit(solution)/shard_map/ppermute | solution.py:18
  61.5 6.0 %pad_maximum_fusion = bf16[6144,512]{1,0:T(8,128)(2,1)} fusion(bf16[2048,512]{1,0:T(8,128)(2,1)} %collective-permute-done.1, bf16[2048,512]{1,0:T(8,128)(2,1)} %param.8, bf16[2048,512]{1,0:T(8,128)(2,1)} %collective-permute-done), kind=kLoop, calls=%fused_computation.4 | loop fusion | flops 18874368 | bytes 12582912 | tf_op jit(solution)/shard_map/concatenate | solution.py:19
  67.5 8.3 %gather_fusion = bf16[64,128,512]{2,1,0:T(8,128)(2,1)} fusion(bf16[48,128,512]{2,1,0:T(8,128)(2,1)} %bitcast.104, s32[1024]{0:T(1024)S(1)} %pad_clamp_fusion), kind=kCustom, calls=%fused_computation | custom fusion | bytes 16777472 | tf_op jit(solution)/shard_map/jit(_take)/gather | solution.py:58
  75.8 7.2 %fusion = f32[16,512,128,1]{1,2,3,0:T(8,128)} fusion(bf16[16,4,128,128]{3,2,1,0:T(8,128)(2,1)S(1)} %copy-done, bf16[16,4,128,512]{3,2,1,0:T(8,128)(2,1)} %bitcast.105, pred[16,4]{1,0:T(8,128)(4,1)S(1)} %copy.13), kind=kOutput, calls=%fused_computation.1 | convolution fusion | flops 1077936128 | bytes 14680128 | tf_op jit(solution)/shard_map/tkab,tkbs->tas/dot_general | solution.py:59
  83.0 162.0 %all-gather.2.cloned.1.call-done = f32[8,2048,512]{2,1,0:T(8,128)} async-done(((f32[1,2048,512]{2,1,0:T(8,128)}), f32[8,2048,512]{2,1,0:T(8,128)}) %all-gather.2.cloned.1.call-update) | async-done | bytes 33554448 | tf_op jit(solution)/shard_map/all_gather | solution.py:66
  245.0 15.1 %reduce_sum.36 = f32[2048,512]{1,0:T(8,128)} reduce(f32[8,2048,512]{2,1,0:T(8,128)} %all-gather.2.cloned.1.call-done, f32[]{:T(128)} %constant.62.clone.1), dimensions={0}, to_apply=%region_0.1 | reduce | flops 7340032 | bytes 37748740 | tf_op jit(solution)/shard_map/reduce_sum | solution.py:66
  260.2 5.7 %fusion.26 = f32[2048,256]{1,0:T(8,128)S(1)} fusion(f32[2048,512]{1,0:T(8,128)} %reduce_sum.36, f32[512,256]{1,0:T(8,128)S(1)} %copy-done.8), kind=kOutput, calls=%fused_computation.77 | convolution fusion | flops 3221225472 | bytes 6815744 | tf_op jit(solution)/shard_map/dot_general | solution.py:28
  265.8 4.1 %multiply_reduce_fusion.2 = (f32[]{:T(128)}, f32[256,256]{1,0:T(8,128)S(1)}) fusion(f32[2048,256]{1,0:T(8,128)S(1)} %fusion.26), kind=kOutput, calls=%fused_computation.50 | convolution fusion | flops 1610743808 | bytes 2359300 | tf_op jit(solution)/shard_map/dot_general | solution.py:28
  275.9 1.9 convolution_divide_fusion
  277.9 4.0 %fusion.34 = f32[256,512]{1,0:T(8,128)S(1)} fusion(f32[2048,256]{1,0:T(8,128)S(1)} %convolution_divide_fusion, f32[2048,512]{1,0:T(8,128)S(1)} %copy-done.2), kind=kOutput, calls=%fused_computation.85 | convolution fusion | flops 3221225472 | bytes 6815744 | tf_op jit(solution)/shard_map/dot_general | solution.py:28
  281.9 1.6 collective-permute-start.2
  283.5 12.6 %collective-permute-done.2 = f32[256,512]{1,0:T(8,128)S(1)} collective-permute-done((f32[256,512]{1,0:T(8,128)S(1)}, f32[256,512]{1,0:T(8,128)S(1)}, u32[]{:S(2)}, u32[]{:S(2)}) %collective-permute-start.2) | collective-permute-done | bytes 524320 | tf_op jit(solution)/shard_map/ppermute | solution.py:24
  296.2 1.0 fusion.7
  297.2 1.6 multiply_reduce_fusion.1
  299.8 0.4 fusion.15
  304.8 0.6 convolution_divide_fusion.2
  305.4 1.1 fusion.6
  306.5 3.3 collective-permute-start.3
  309.8 11.8 %collective-permute-done.3 = f32[256,512]{1,0:T(8,128)S(1)} collective-permute-done((f32[256,512]{1,0:T(8,128)S(1)}, f32[256,512]{1,0:T(8,128)S(1)}, u32[]{:S(2)}, u32[]{:S(2)}) %collective-permute-start.3) | collective-permute-done | bytes 524320 | tf_op jit(solution)/shard_map/ppermute | solution.py:24
  321.7 2.0 fusion.5
  323.7 1.6 multiply_reduce_fusion
  326.4 0.4 fusion.16
  329.8 1.1 fusion.47
  331.3 1.5 select_subtract_fusion
  333.2 1.6 convolution_divide_fusion.1
  334.8 1.8 fusion.4
  336.6 1.3 fusion.8
  338.4 4.5 %fusion.49 = f32[2048,64]{0,1:T(8,128)} fusion(f32[2048,256]{1,0:T(8,128)} %copy-done.3, f32[256,64]{0,1:T(8,128)S(1)} %fusion.17), kind=kOutput, calls=%fused_computation.100 | convolution fusion | flops 402653184 | bytes 2686976 | tf_op jit(solution)/shard_map/dot_general | solution.py:28
  (65 shorter events, 14.9 us)
Async XLA Ops:
  7.2 68.6 %copy-start = (bf16[16,4,128,128]{3,2,1,0:T(8,128)(2,1)S(1)}, bf16[16,4,128,128]{3,2,1,0:T(8,128)(2,1)}, u32[]{:S(2)}) copy-start(bf16[16,4,128,128]{3,2,1,0:T(8,128)(2,1)} %param.6) | copy-start | bytes 6291460
  7.2 237.9 %all-gather.2.cloned.1.call-start = ((), (), s32[]{:S(2)}) async-start(), calls=%async_computation | async-start | bytes 37748736 | tf_op jit(solution)/shard_map/all_gather | solution.py:66
  7.2 48.8 %collective-permute-start = (bf16[2048,512]{1,0:T(8,128)(2,1)}, bf16[2048,512]{1,0:T(8,128)(2,1)}, u32[]{:S(2)}, u32[]{:S(2)}) collective-permute-start(bf16[2048,512]{1,0:T(8,128)(2,1)} %param.8), channel_id=1, source_target_pairs={{0,8},{8,16},{16,24},{24,32},{32,40},{40,48},{48,56},{56,64},{64,7... | collective-permute-start | bytes 6291464 | tf_op jit(solution)/shard_map/ppermute | solution.py:15
  12.2 49.3 %collective-permute-start.1 = (bf16[2048,512]{1,0:T(8,128)(2,1)}, bf16[2048,512]{1,0:T(8,128)(2,1)}, u32[]{:S(2)}, u32[]{:S(2)}) collective-permute-start(bf16[2048,512]{1,0:T(8,128)(2,1)} %param.8), channel_id=1, source_target_pairs={{8,0},{16,8},{24,16},{32,24},{40,32},{48,40},{56,48},{64,56},{72,6... | collective-permute-start | bytes 6291464 | tf_op jit(solution)/shard_map/ppermute | solution.py:18
  83.0 177.2 %copy-start.8 = (f32[512,256]{1,0:T(8,128)S(1)}, f32[512,256]{1,0:T(8,128)}, u32[]{:S(2)}) copy-start(f32[512,256]{1,0:T(8,128)} %param.9) | copy-start | bytes 1572868
  275.5 2.3 copy-start.2
  277.9 4.0 %copy-start.3 = (f32[2048,256]{1,0:T(8,128)}, f32[2048,256]{1,0:T(8,128)S(1)}, u32[]{:S(2)}) copy-start(f32[2048,256]{1,0:T(8,128)S(1)} %convolution_divide_fusion) | copy-start | bytes 6291460
  277.9 18.3 %copy-start.7 = (f32[512,256]{1,0:T(8,128)S(1)}, f32[512,256]{1,0:T(8,128)}, u32[]{:S(2)}) copy-start(f32[512,256]{1,0:T(8,128)} %param.10) | copy-start | bytes 1572868
  281.9 14.2 %collective-permute-start.2 = (f32[256,512]{1,0:T(8,128)S(1)}, f32[256,512]{1,0:T(8,128)S(1)}, u32[]{:S(2)}, u32[]{:S(2)}) collective-permute-start(f32[256,512]{1,0:T(8,128)S(1)} %fusion.34), channel_id=1, source_target_pairs={{0,8},{8,0},{16,24},{24,16},{32,40},{40,32},{48,56},{56,48},{64,72... | collective-permute-start | bytes 1572872 | tf_op jit(solution)/shard_map/ppermute | solution.py:24
  305.4 21.0 %copy-start.5 = (f32[512,256]{1,0:T(8,128)}, f32[512,256]{1,0:T(8,128)S(1)}, u32[]{:S(2)}) copy-start(f32[512,256]{1,0:T(8,128)S(1)} %convolution_divide_fusion.2) | copy-start | bytes 1572868
  306.5 15.1 %collective-permute-start.3 = (f32[256,512]{1,0:T(8,128)S(1)}, f32[256,512]{1,0:T(8,128)S(1)}, u32[]{:S(2)}, u32[]{:S(2)}) collective-permute-start(f32[256,512]{1,0:T(8,128)S(1)} %fusion.6), channel_id=1, source_target_pairs={{0,16},{8,24},{16,0},{24,8},{32,48},{40,56},{48,32},{56,40},{64,80... | collective-permute-start | bytes 1572872 | tf_op jit(solution)/shard_map/ppermute | solution.py:24
  323.7 5.7 %copy-start.4 = (f32[512,256]{1,0:T(8,128)}, f32[512,256]{1,0:T(8,128)S(1)}, u32[]{:S(2)}) copy-start(f32[512,256]{1,0:T(8,128)S(1)} %fusion.5) | copy-start | bytes 1572868
  331.3 11.6 %copy-start.1 = (bf16[16,4,128,128]{3,2,1,0:T(8,128)(2,1)S(1)}, bf16[16,4,128,128]{3,2,1,0:T(8,128)(2,1)}, u32[]{:S(2)}) copy-start(bf16[16,4,128,128]{3,2,1,0:T(8,128)(2,1)} %param.6) | copy-start | bytes 6291460
  338.0 4.9 %copy-start.6 = (f32[256,256]{1,0:T(8,128)}, f32[256,256]{1,0:T(8,128)S(1)}, u32[]{:S(2)}) copy-start(f32[256,256]{1,0:T(8,128)S(1)} %fusion.8) | copy-start | bytes 786436
Sparse Core Ops, SparseCore 0:
  83.1 161.8 all-gather.1
